TPU v7x, 32 devices: a whole 2x2x4 slice. The times are simulated.
32 devices in a mesh: lon: 8 (over y, x, core), mem: 4 (over z).
Axes of the slice: x: 2, y: 2, z: 4, core: 2. Of those that a mesh axis runs over, the one named last changes fastest.
Arguments:
- sample_collection: bfloat16 [256, 3, 1, 16, 1024], P('mem', None, None, None, 'lon'), may hold values from -6 to 6
- layer_depth: float32 [1, 16, 1024], P(None, None, 'lon'), may hold values from 0.05 to 0.2
- obs_where: int32 [4, 8, 512], P('mem', 'lon'), may hold values from 0 to 4895, as said below
- observed_values: float32 [4, 8, 512], P('mem', 'lon'), may hold values from -6 to 6
- obs_precision: float32 [4, 8, 512], P('mem', 'lon'), may hold values from 0.5 to 4
- loc_index: int32 [4, 8, 512], P('mem', 'lon'), may hold values from 0 to 15
- obs_count: int32 [4, 8], P('mem', 'lon'), may hold values from 64 to 512, as said below
Outputs:
- analysis: bfloat16 [256, 3, 1, 16, 1024], P('mem', None, None, None, 'lon')
Inputs may be any that keep to these rules, and one draw needn't show every extreme that they name: `obs_where`: flat index into a block's region of 3 x 1 x (12) x (136) cells (component, layer, row, column). Slots o < obs_count of a block hold observations; in each draw some block has all 512.
All inputs are finite; a program needn't handle non-finite values.
Results may differ from a plain program's by a relative error of at most 0.0037.
The roundings to bfloat16 on the way count: a program that leaves them out, or rounds other values in their place, can miss the bound.
Values may be sent and summed in bfloat16 or wider, within the bound.
A program may use at most 128 MiB of HBM per device.

v0:
```python
import functools
import math

import jax
import jax.numpy as jnp
from jax import lax
from jax.experimental import pallas as pl
from jax.experimental.pallas import tpu as pltpu
from jax.sharding import PartitionSpec as P

STEPS = 2
MARGIN_WIDTH = 4
BAND = 4
NS_ITERS = 5
EDGE = 8
CHUNK = 16
MESH = pl.DeviceIdType.MESH
HIGHEST = lax.Precision.HIGHEST

time_step = 0.8
inflation = 1.1
half_step = 0.5 * time_step


def iota(shape, axis):
    return lax.broadcasted_iota(jnp.int32, shape, axis)


def xor(me, mask):
    out = me
    bit = 1
    while bit <= mask:
        if mask & bit:
            out = out + bit - 2 * bit * lax.rem(me // bit, 2)
        bit *= 2
    return out


def spin(row, count_rows):
    return 0.4 * (row / (count_rows - 1) - 0.5)


def forecast_rows(h, u, v, depth):
    rows = len(h)
    wide = h[0].shape[-1]
    for _ in range(STEPS):
        flux_east = [depth[r] * u[r] for r in range(rows)]
        flux_north = [depth[r] * v[r] for r in range(rows)]
        h_new = []
        for r in range(rows):
            change = pltpu.roll(flux_east[r], wide - 1, 1) - pltpu.roll(flux_east[r], 1, 1)
            if r + 1 < rows:
                change = change + flux_north[r + 1]
            if r > 0:
                change = change - flux_north[r - 1]
            h_new.append(h[r] - half_step * change)
        u_new, v_new = [], []
        for r in range(rows):
            turn = time_step * spin(r, rows)
            slope = pltpu.roll(h_new[r], wide - 1, 1) - pltpu.roll(h_new[r], 1, 1)
            u_new.append(u[r] - half_step * slope + turn * v[r])
            new = v[r] - turn * u[r]
            if r + 1 < rows:
                new = new - half_step * h_new[r + 1]
            if r > 0:
                new = new + half_step * h_new[r - 1]
            v_new.append(new)
        h, u, v = h_new, u_new, v_new
    return h, u, v


def forecast_edge(left, right, depth_left, depth_right, rows):
    lanes = rows * EDGE
    at = iota((1, lanes), 1)
    place = lax.rem(at, EDGE)
    row = at // EDGE
    turn = time_step * 0.4 * (row.astype(jnp.float32) / (rows - 1) - 0.5)

    def shift(x, by):
        return pltpu.roll(x, by % lanes, 1)

    def lon(x_left, x_right):
        d_left = jnp.where(place == EDGE - 1, shift(x_right, EDGE - 1), shift(x_left, -1)) - shift(x_left, 1)
        d_right = shift(x_right, -1) - jnp.where(place == 0, shift(x_left, 1 - EDGE), shift(x_right, 1))
        return d_left, d_right

    def lat(x):
        north = jnp.where(row == rows - 1, 0.0, shift(x, -EDGE))
        south = jnp.where(row == 0, 0.0, shift(x, EDGE))
        return north - south

    for _ in range(STEPS):
        (h_l, u_l, v_l), (h_r, u_r, v_r) = left, right
        d_l, d_r = lon(depth_left * u_l, depth_right * u_r)
        n_l = h_l - half_step * (d_l + lat(depth_left * v_l))
        n_r = h_r - half_step * (d_r + lat(depth_right * v_r))
        s_l, s_r = lon(n_l, n_r)
        left = (n_l, u_l - half_step * s_l + turn * v_l, v_l - half_step * lat(n_l) - turn * u_l)
        right = (n_r, u_r - half_step * s_r + turn * v_r, v_r - half_step * lat(n_r) - turn * u_r)
    return left, right


def pack_depth(depth, side, strip):
    rows = depth.shape[0]
    lanes = rows * EDGE
    at = iota((1, lanes), 1)
    source = lax.rem(at, EDGE) + side * (strip - EDGE)
    spread = jnp.where(iota((strip, lanes), 0) == source, 1.0, 0.0)
    copies = jnp.dot(depth, spread, precision=HIGHEST, preferred_element_type=jnp.float32)
    kept = jnp.where(iota((rows, lanes), 0) == at // EDGE, copies, 0.0)
    return jnp.sum(kept, axis=0, keepdims=True)


def kernel(
    n, lons,
    x_ref, depth_ref, where_ref, values_ref, precision_ref, loc_ref, count_ref, out_ref,
    tall32, flat16, main32, edge_lo, edge_hi, west_hi, east_lo, depth_west, depth_east,
    wheres, fore, halo, cells, picks, picked, transform, result, back, out32,
    side_send, side_recv, where_send, where_recv, cell_send, cell_recv,
    pick_send, pick_recv, back_send, back_recv,
):
    me = lax.axis_index("mem")
    here = lax.axis_index("lon")
    east = lax.rem(here + 1, lons)
    west = lax.rem(here + lons - 1, lons)
    group, _, _, rows, strip = x_ref.shape
    members = n * group
    slots = where_ref.shape[-1]
    wide = strip + 2 * MARGIN_WIDTH
    band_rows = BAND + 2 * MARGIN_WIDTH
    area = band_rows * wide
    cell = BAND * strip
    lanes = rows * EDGE
    stack = 3 * rows
    masks = list(range(n - 1, 0, -1))
    peers = {mask: xor(me, mask) for mask in masks}

    barrier = pltpu.get_barrier_semaphore()
    for mask in masks:
        pl.semaphore_signal(barrier, inc=1, device_id={"mem": peers[mask]}, device_id_type=MESH)
    pl.semaphore_signal(barrier, inc=1, device_id={"lon": east}, device_id_type=MESH)
    pl.semaphore_signal(barrier, inc=1, device_id={"lon": west}, device_id_type=MESH)

    tall32[...] = x_ref[...].reshape(group * stack, strip).astype(jnp.float32)
    for c in range(3):
        for r in range(rows):
            row = tall32[pl.ds(c * rows + r, group, stride=stack), :]
            flat16[pl.ds(c * group, group), pl.ds(r * strip, strip)] = row.astype(jnp.bfloat16)

    per = min(rows, 128 // EDGE)
    at = iota((1, 2 * per * EDGE), 1)
    inner = lax.rem(at, per * EDGE)
    source = (inner // EDGE) * strip + lax.rem(inner, EDGE) + (at // (per * EDGE)) * (strip - EDGE)
    choose = jnp.where(iota((per * strip, 2 * per * EDGE), 0) == source, 1.0, 0.0).astype(jnp.bfloat16)
    for t in range(rows // per):
        part = jnp.dot(
            flat16[:, pl.ds(t * per * strip, per * strip)], choose, preferred_element_type=jnp.float32
        ).astype(jnp.bfloat16)
        edge_lo[:, pl.ds(t * per * EDGE, per * EDGE)] = part[:, : per * EDGE]
        edge_hi[:, pl.ds(t * per * EDGE, per * EDGE)] = part[:, per * EDGE :]

    pl.semaphore_wait(barrier, n + 1)

    def to_lon(src, dst, i, peer):
        return pltpu.make_async_remote_copy(
            src_ref=src, dst_ref=dst, send_sem=side_send.at[i], recv_sem=side_recv.at[i],
            device_id={"lon": peer}, device_id_type=MESH,
        )

    def to_mem(src, dst, ss, rs, mask):
        return pltpu.make_async_remote_copy(
            src_ref=src, dst_ref=dst, send_sem=ss, recv_sem=rs,
            device_id={"mem": peers[mask]}, device_id_type=MESH,
        )

    side_copies = [
        to_lon(edge_hi, west_hi, 0, east),
        to_lon(edge_lo, east_lo, 1, west),
        to_lon(depth_ref, depth_west, 2, east),
        to_lon(depth_ref, depth_east, 3, west),
    ]
    where_copies = [
        to_mem(where_ref, wheres.at[me], where_send.at[mask], where_recv.at[mask], mask) for mask in masks
    ]
    for copy in side_copies + where_copies:
        copy.start()
    wheres[me] = where_ref[...]

    @pl.loop(0, group // CHUNK)
    def _(i):
        base = i * (CHUNK * stack)
        state = [
            [tall32[pl.ds(base + c * rows + r, CHUNK, stride=stack), :] for r in range(rows)] for c in range(3)
        ]
        depth = [depth_ref[pl.ds(r, 1), :] for r in range(rows)]
        some = pl.ds(pl.multiple_of(i * CHUNK, CHUNK), CHUNK)
        for c, field in enumerate(forecast_rows(*state, depth)):
            for r in range(rows):
                main32[c * rows + r, some, :] = field[r]

    own_lo = pack_depth(depth_ref[...], 0, strip)
    own_hi = pack_depth(depth_ref[...], 1, strip)
    for copy in side_copies:
        copy.wait_recv()
    far_hi = pack_depth(depth_west[...], 1, strip)
    far_lo = pack_depth(depth_east[...], 0, strip)

    @pl.loop(0, group // CHUNK)
    def _(i):
        begin = pl.multiple_of(i * CHUNK, CHUNK)
        some = pl.ds(begin, CHUNK)

        def edge(ref):
            return [
                ref[pl.ds(pl.multiple_of(c * group + begin, CHUNK), CHUNK), :].astype(jnp.float32) for c in range(3)
            ]

        w_left, w_right = forecast_edge(edge(west_hi), edge(edge_lo), far_hi, own_lo, rows)
        e_left, e_right = forecast_edge(edge(edge_hi), edge(east_lo), own_hi, far_lo, rows)
        place = lax.rem(iota((1, lanes), 1), EDGE)
        column = iota((1, strip), 1)
        for c in range(3):
            outer = jnp.where(place >= MARGIN_WIDTH, w_left[c], e_right[c])
            halo[pl.ds(pl.multiple_of(c * group + begin, CHUNK), CHUNK), :] = outer.astype(jnp.bfloat16)
            rim = jnp.where(place < MARGIN_WIDTH, w_right[c], e_left[c])
            for t in range(rows // per):
                tile = rim[:, t * per * EDGE : (t + 1) * per * EDGE]
                turned = [tile] + [pltpu.roll(tile, (per - q) * EDGE, 1) for q in range(1, per)]
                for q in range(per):
                    r = t * per + q
                    value = main32[c * rows + r, some, :]
                    value = jnp.where(column < MARGIN_WIDTH, turned[q], value)
                    value = jnp.where(column >= strip - MARGIN_WIDTH, turned[(q + 1) % per], value)
                    fore[r // BAND, c, some, pl.ds((r % BAND) * strip, strip)] = value.astype(jnp.bfloat16)

    cell_copies = [
        [
            to_mem(fore.at[peers[mask], c], cells.at[c, me], cell_send.at[c, mask], cell_recv.at[c, mask], mask)
            for mask in masks
        ]
        for c in range(3)
    ]
    for copy in cell_copies[0]:
        copy.start()

    for copy in where_copies:
        copy.wait_recv()
    pick_copies = []
    for mask in masks + [0]:
        band = peers[mask] if mask else me
        index = wheres[band]
        component = jnp.where(index >= area, 1, 0) + jnp.where(index >= 2 * area, 1, 0)
        rest = index - component * area
        row = jnp.zeros_like(rest)
        for q in range(1, band_rows):
            row = row + jnp.where(rest >= q * wide, 1, 0)
        column = rest - row * wide - MARGIN_WIDTH
        block = jnp.where(row >= BAND, 1, 0) + jnp.where(row >= 2 * BAND, 1, 0)
        inside = jnp.logical_and(column >= 0, column < strip)
        target = jnp.where(inside, (row - block * BAND) * strip + column, -1)
        place = jnp.where(column < 0, column + EDGE, column - strip)
        rim_target = jnp.where(inside, -1, (band * BAND - MARGIN_WIDTH + row) * EDGE + place)
        hot = jnp.where(iota((cell, slots), 0) == target, 1.0, 0.0).astype(jnp.bfloat16)
        rim_hot = jnp.where(iota((lanes, slots), 0) == rim_target, 1.0, 0.0).astype(jnp.bfloat16)
        parts = [(c, e) for c in range(3) for e in range(3)]
        table = jnp.concatenate([fore[lax.rem(band + e + n - 1, n), c] for c, e in parts], axis=0)
        found = jnp.dot(table, hot, preferred_element_type=jnp.float32)
        rim_found = jnp.dot(halo[...], rim_hot, preferred_element_type=jnp.float32)
        total = jnp.zeros((group, slots), jnp.float32)
        for q, (c, e) in enumerate(parts):
            exists = jnp.logical_and(band + e - 1 >= 0, band + e - 1 < n)
            wanted = jnp.where(exists, 3 * c + e, -1)
            total = jnp.where(3 * component + block == wanted, found[q * group : (q + 1) * group], total)
        for c in range(3):
            rim_part = rim_found[c * group : (c + 1) * group]
            total = total + jnp.where(component == c, rim_part, 0.0)
        if mask:
            picks[mask] = total.astype(jnp.bfloat16)
            copy = to_mem(picks.at[mask], picked.at[me], pick_send.at[mask], pick_recv.at[mask], mask)
            copy.start()
            pick_copies.append(copy)
        else:
            picked[me] = total.astype(jnp.bfloat16)

    for c in range(1, 3):
        for copy in cell_copies[c]:
            copy.start()
    for c in range(3):
        cells[c, me] = fore[me, c]

    live = jnp.where(iota((1, slots), 1) < count_ref[...], 1.0, 0.0)
    taper = 1.0 - loc_ref[...].astype(jnp.float32) / 16.0
    weight = precision_ref[...] * (taper * taper) * live

    for copy in pick_copies:
        copy.wait_recv()
    obs = picked[...].astype(jnp.float32).reshape(members, slots)
    obs_mean = jnp.mean(obs, axis=0, keepdims=True)
    spread = obs - obs_mean
    weighted = spread * weight
    innovation = values_ref[...] - obs_mean

    def mm(a, b):
        return jnp.dot(a, b, precision=HIGHEST, preferred_element_type=jnp.float32)

    gram = lax.dot_general(
        weighted, spread, (((1,), (1,)), ((), ())),
        precision=HIGHEST, preferred_element_type=jnp.float32,
    )
    drive = jnp.sum(weighted * innovation, axis=1, keepdims=True)
    prior = (members - 1) / inflation
    trace = jnp.sum(jnp.sum(weighted * spread, axis=1, keepdims=True), axis=0, keepdims=True)
    trace_bound = prior + trace
    identity = jnp.where(iota((members, members), 0) == iota((members, members), 1), 1.0, 0.0)
    root_iter = (gram + prior * identity) / trace_bound
    correction = 1.5 * identity - 0.5 * root_iter
    root_iter = mm(root_iter, correction)
    inv_root = correction
    for sweep in range(1, NS_ITERS):
        correction = 1.5 * identity - 0.5 * mm(inv_root, root_iter)
        if sweep < NS_ITERS - 1:
            root_iter = mm(root_iter, correction)
        inv_root = mm(correction, inv_root)
    shrink = inv_root * lax.rsqrt(trace_bound)
    inner = jnp.sum(shrink * drive, axis=0, keepdims=True)
    mean_weight = jnp.sum(shrink * inner, axis=1, keepdims=True)
    weights = math.sqrt(members - 1) * shrink + mean_weight
    weights = weights + (1.0 - jnp.sum(weights, axis=0, keepdims=True)) / members
    weights_t = weights.T
    high = weights_t.astype(jnp.bfloat16)
    transform[0] = high
    transform[1] = (weights_t - high.astype(jnp.float32)).astype(jnp.bfloat16)

    back_copies = []
    for c in range(3):
        for copy in cell_copies[c]:
            copy.wait_recv()
        all_cells = cells[c].reshape(members, cell)
        total = jnp.dot(transform[0], all_cells, preferred_element_type=jnp.float32)
        total += jnp.dot(transform[1], all_cells, preferred_element_type=jnp.float32)
        result[c] = total.astype(jnp.bfloat16).reshape(n, group, cell)
        row_copies = [
            to_mem(result.at[c, peers[mask]], back.at[c, me], back_send.at[c, mask], back_recv.at[c, mask], mask)
            for mask in masks
        ]
        for copy in row_copies:
            copy.start()
        back_copies.append(row_copies)
        back[c, me] = result[c, me]

    def place_rows(c, band):
        block = back[c, band].astype(jnp.float32)
        for q in range(BAND):
            out32[c, pl.ds(band * BAND + q, group, stride=rows), :] = block[:, q * strip : (q + 1) * strip]

    for c in range(3):
        place_rows(c, me)
        for copy, mask in zip(back_copies[c], masks):
            copy.wait_recv()
            place_rows(c, peers[mask])
        out_ref[:, c, 0] = out32[c].reshape(group, rows, strip).astype(jnp.bfloat16)

    for copy in side_copies + where_copies + pick_copies:
        copy.wait_send()
    for c in range(3):
        for copy in cell_copies[c] + back_copies[c]:
            copy.wait_send()


def on_device(
    sample_collection, layer_depth, obs_where, observed_values, obs_precision, loc_index, obs_count
):
    n, lons = lax.axis_size("mem"), lax.axis_size("lon")
    group, _, _, rows, strip = sample_collection.shape
    slots = obs_where.shape[-1]
    members, lanes, cell = n * group, rows * EDGE, BAND * strip
    vmem = pl.BlockSpec(memory_space=pltpu.VMEM)
    dma = pltpu.SemaphoreType.DMA
    f32, bf16 = jnp.float32, jnp.bfloat16
    scratch = [
        pltpu.VMEM((group * 3 * rows, strip), f32),
        pltpu.VMEM((3 * group, rows * strip), bf16),
        pltpu.VMEM((3 * rows, group, strip), f32),
    ]
    scratch += [pltpu.VMEM((3 * group, lanes), bf16)] * 4
    scratch += [pltpu.VMEM((rows, strip), f32)] * 2
    scratch += [
        pltpu.VMEM((n, 1, slots), jnp.int32),
        pltpu.VMEM((n, 3, group, cell), bf16),
        pltpu.VMEM((3 * group, lanes), bf16),
        pltpu.VMEM((3, n, group, cell), bf16),
        pltpu.VMEM((n, group, slots), bf16),
        pltpu.VMEM((n, group, slots), bf16),
        pltpu.VMEM((2, members, members), bf16),
        pltpu.VMEM((3, n, group, cell), bf16),
        pltpu.VMEM((3, n, group, cell), bf16),
        pltpu.VMEM((3, group * rows, strip), f32),
    ]
    scratch += [dma((4,))] * 2 + [dma((n,))] * 2 + [dma((3, n))] * 2 + [dma((n,))] * 2 + [dma((3, n))] * 2
    return pl.pallas_call(
        functools.partial(kernel, n, lons),
        out_shape=jax.ShapeDtypeStruct(sample_collection.shape, bf16),
        in_specs=[vmem] * 7,
        out_specs=vmem,
        scratch_shapes=scratch,
        compiler_params=pltpu.CompilerParams(
            collective_id=0, has_side_effects=True, vmem_limit_bytes=60 * 1024 * 1024
        ),
    )(
        sample_collection, layer_depth[0], obs_where[0], observed_values[0],
        obs_precision[0], loc_index[0], obs_count,
    )


def solution(mesh):
    in_specs = (
        P("mem", None, None, None, "lon"),
        P(None, None, "lon"),
        P("mem", "lon", None),
        P("mem", "lon", None),
        P("mem", "lon", None),
        P("mem", "lon", None),
        P("mem", "lon"),
    )
    out_specs = P("mem", None, None, None, "lon")
    return jax.shard_map(
        on_device, mesh=mesh, in_specs=in_specs, out_specs=out_specs, check_vma=False
    )
```

profile of v0, /device:TPU:0, one launch (start us, length us, event | category | flops | bytes accessed | tf_op | source)
XLA Modules:
  0.0 57.4 jit_solution(17300170639590841322)
XLA Ops:
  0.7 54.7 %shard_map.73 = bf16[64,3,1,16,128]{4,3,2,1,0:T(8,128)(2,1)} custom-call(bf16[64,3,1,16,128]{4,3,2,1,0:T(8,128)(2,1)} %x_ref.1, f32[16,128]{1,0:T(8,128)} %bitcast.5, s32[1,512]{1,0:T(1,128)} %bitcast.6, f32[1,512]{1,0:T(1,128)} %bitcast.7, f32[1,512]{1,0:T(1,128)} %bitcast.8, s32[1,512]{1,0:T(1,128)} %bitcast.9, s32[1,1]{1,0:T(1,128)S(6)} %copy.9.count_ref), custom_call_target="tpu_custom_call" | custom-call | tf_op jit(solution)/shard_map/pallas_call | solution.py:400
  55.3 2.1 %copy.10 = bf16[64,3,1,16,128]{4,3,2,1,0:T(8,128)(2,1)} copy(bf16[64,3,1,16,128]{4,3,2,1,0:T(8,128)(2,1)} %shard_map.73) | data formatting | bytes 1572864
where the time goes:
time: 57.6 us; the launch traced here: 57.4 us
  Pallas kernels  54.7 us (95%)
  local copies, waits for them, and re-layouts  2.09 us (4%)
  between operations  0.66 us (1%)
    pallas_call x1, Pallas kernels, on_device(): pl.pallas_call(functools.partial(kernel, n, lons), out_shape=jax.ShapeDty...  54.7 us
    unnamed x1, local copies, waits for them, and re-layouts  2.09 us

commit v1 on v0

--- a/solution.py
+++ b/solution.py
@@ -113,9 +113,9 @@
 
 def kernel(
     n, lons,
-    x_ref, depth_ref, where_ref, values_ref, precision_ref, loc_ref, count_ref, out_ref,
-    tall32, flat16, main32, edge_lo, edge_hi, west_hi, east_lo, depth_west, depth_east,
-    wheres, fore, halo, cells, picks, picked, transform, result, back, out32,
+    x_hbm, depth_hbm, where_hbm, values_hbm, precision_hbm, loc_hbm, count_hbm, out_ref,
+    x_ref, depth_ref, values_ref, precision_ref, loc_ref, count_ref, tall32, flat16, main32, edge_lo, edge_hi, west_hi, east_lo, depth_west, depth_east,
+    wheres, fore, halo, cells, picks, picked, transform, result, back, out32, local_sem,
     side_send, side_recv, where_send, where_recv, cell_send, cell_recv,
     pick_send, pick_recv, back_send, back_recv,
 ):
@@ -125,7 +125,7 @@
     west = lax.rem(here + lons - 1, lons)
     group, _, _, rows, strip = x_ref.shape
     members = n * group
-    slots = where_ref.shape[-1]
+    slots = where_hbm.shape[-1]
     wide = strip + 2 * MARGIN_WIDTH
     band_rows = BAND + 2 * MARGIN_WIDTH
     area = band_rows * wide
@@ -134,6 +134,13 @@
     stack = 3 * rows
     masks = list(range(n - 1, 0, -1))
     peers = {mask: xor(me, mask) for mask in masks}
+    local_copies = [
+        pltpu.make_async_copy(src, dst, local_sem.at[i])
+        for i, (src, dst) in enumerate([
+            (x_hbm, x_ref), (depth_hbm, depth_ref), (where_hbm, wheres.at[me]), (values_hbm, values_ref),
+            (precision_hbm, precision_ref), (loc_hbm, loc_ref), (count_hbm, count_ref),
+        ])
+    ]
 
     barrier = pltpu.get_barrier_semaphore()
     for mask in masks:
@@ -141,6 +148,10 @@
     pl.semaphore_signal(barrier, inc=1, device_id={"lon": east}, device_id_type=MESH)
     pl.semaphore_signal(barrier, inc=1, device_id={"lon": west}, device_id_type=MESH)
 
+    for copy in local_copies:
+        copy.start()
+
+    local_copies[0].wait()
     tall32[...] = x_ref[...].reshape(group * stack, strip).astype(jnp.float32)
     for c in range(3):
         for r in range(rows):
@@ -176,15 +187,16 @@
     side_copies = [
         to_lon(edge_hi, west_hi, 0, east),
         to_lon(edge_lo, east_lo, 1, west),
-        to_lon(depth_ref, depth_west, 2, east),
-        to_lon(depth_ref, depth_east, 3, west),
+        to_lon(depth_hbm, depth_west, 2, east),
+        to_lon(depth_hbm, depth_east, 3, west),
     ]
     where_copies = [
-        to_mem(where_ref, wheres.at[me], where_send.at[mask], where_recv.at[mask], mask) for mask in masks
+        to_mem(where_hbm, wheres.at[me], where_send.at[mask], where_recv.at[mask], mask) for mask in masks
     ]
     for copy in side_copies + where_copies:
         copy.start()
-    wheres[me] = where_ref[...]
+
+    local_copies[1].wait()
 
     @pl.loop(0, group // CHUNK)
     def _(i):
@@ -245,6 +257,7 @@
 
     for copy in where_copies:
         copy.wait_recv()
+    local_copies[2].wait()
     pick_copies = []
     for mask in masks + [0]:
         band = peers[mask] if mask else me
@@ -288,6 +301,8 @@
     for c in range(3):
         cells[c, me] = fore[me, c]
 
+    for copy in local_copies[3:]:
+        copy.wait()
     live = jnp.where(iota((1, slots), 1) < count_ref[...], 1.0, 0.0)
     taper = 1.0 - loc_ref[...].astype(jnp.float32) / 16.0
     weight = precision_ref[...] * (taper * taper) * live
@@ -367,6 +382,12 @@
             copy.wait_send()
 
 
+def deliver(in_ref, out_ref, sem):
+    copy = pltpu.make_async_copy(in_ref, out_ref, sem)
+    copy.start()
+    copy.wait()
+
+
 def on_device(
     sample_collection, layer_depth, obs_where, observed_values, obs_precision, loc_index, obs_count
 ):
@@ -378,6 +399,12 @@
     dma = pltpu.SemaphoreType.DMA
     f32, bf16 = jnp.float32, jnp.bfloat16
     scratch = [
+        pltpu.VMEM(sample_collection.shape, bf16),
+        pltpu.VMEM((rows, strip), f32),
+        pltpu.VMEM((1, slots), f32),
+        pltpu.VMEM((1, slots), f32),
+        pltpu.VMEM((1, slots), jnp.int32),
+        pltpu.VMEM((1, 1), jnp.int32),
         pltpu.VMEM((group * 3 * rows, strip), f32),
         pltpu.VMEM((3 * group, rows * strip), bf16),
         pltpu.VMEM((3 * rows, group, strip), f32),
@@ -396,11 +423,12 @@
         pltpu.VMEM((3, n, group, cell), bf16),
         pltpu.VMEM((3, group * rows, strip), f32),
     ]
+    scratch += [dma((7,))]
     scratch += [dma((4,))] * 2 + [dma((n,))] * 2 + [dma((3, n))] * 2 + [dma((n,))] * 2 + [dma((3, n))] * 2
-    return pl.pallas_call(
+    out = pl.pallas_call(
         functools.partial(kernel, n, lons),
-        out_shape=jax.ShapeDtypeStruct(sample_collection.shape, bf16),
-        in_specs=[vmem] * 7,
+        out_shape=pltpu.VMEM(sample_collection.shape, bf16),
+        in_specs=[pl.BlockSpec(memory_space=pltpu.HBM)] * 7,
         out_specs=vmem,
         scratch_shapes=scratch,
         compiler_params=pltpu.CompilerParams(
@@ -410,6 +438,14 @@
         sample_collection, layer_depth[0], obs_where[0], observed_values[0],
         obs_precision[0], loc_index[0], obs_count,
     )
+    return pl.pallas_call(
+        deliver,
+        out_shape=jax.ShapeDtypeStruct(sample_collection.shape, bf16),
+        in_specs=[vmem],
+        out_specs=pl.BlockSpec(memory_space=pl.ANY),
+        scratch_shapes=[dma(())],
+        compiler_params=pltpu.CompilerParams(vmem_limit_bytes=4 * 1024 * 1024),
+    )(out)
 
 
 def solution(mesh):

time: 57.6 us -> 54.8 us (0.951)
  local copies, waits for them, and re-layouts: 2.09 us -> 0 us
  Pallas kernels: 54.7 us -> 54 us
    unnamed x1 -> x0, local copies, waits for them, and re-layouts: 2.09 us -> none
    pallas_call x1 -> x2, Pallas kernels: 54.7 us -> 54 us  [the longest x1 53.1 us: on_device(): pl.pallas_call(functools.partial(kernel, n, lons), out_shape=pltpu.VMEM(s...]
where the time goes in v1:
time: 54.8 us; the launch traced here: 54.6 us
  Pallas kernels  54 us (99%)
  between operations  0.66 us (1%)
    pallas_call x1, Pallas kernels, on_device(): pl.pallas_call(functools.partial(kernel, n, lons), out_shape=pltpu.VMEM(s...  53.1 us

profile of v1, /device:TPU:0, one launch (start us, length us, event | category | flops | bytes accessed | tf_op | source)
XLA Modules:
  0.0 54.6 jit_solution(16425704792653235565)
XLA Ops:
  0.7 53.1 %shard_map.73.in_ref = bf16[64,3,1,16,128]{4,3,2,1,0:T(8,128)(2,1)S(1)} custom-call(bf16[64,3,1,16,128]{4,3,2,1,0:T(8,128)(2,1)} %x_hbm.1, f32[16,128]{1,0:T(8,128)} %bitcast.5, s32[1,512]{1,0:T(1,128)} %bitcast.6, f32[1,512]{1,0:T(1,128)} %bitcast.7, f32[1,512]{1,0:T(1,128)} %bitcast.8, s32[1,512]{1,0:T(1,128)} %bitcast.9, s32[1,1]{1,0:T(1,128)S(6)} %copy.8.count_hbm), custom_call_target="tpu_custom_call" | custom-call | tf_op jit(solution)/shard_map/pallas_call | solution.py:428
  53.8 0.9 %shard_map.74 = bf16[64,3,1,16,128]{4,3,2,1,0:T(8,128)(2,1)} custom-call(bf16[64,3,1,16,128]{4,3,2,1,0:T(8,128)(2,1)S(1)} %shard_map.73.in_ref), custom_call_target="tpu_custom_call" | custom-call | tf_op jit(solution)/shard_map/pallas_call | solution.py:441

commit v2 on v1

--- a/solution.py
+++ b/solution.py
@@ -114,9 +114,9 @@
 def kernel(
     n, lons,
     x_hbm, depth_hbm, where_hbm, values_hbm, precision_hbm, loc_hbm, count_hbm, out_ref,
-    x_ref, depth_ref, values_ref, precision_ref, loc_ref, count_ref, tall32, flat16, main32, edge_lo, edge_hi, west_hi, east_lo, depth_west, depth_east,
+    x_ref, depth_ref, values_ref, precision_ref, loc_ref, count_ref, tall32, flat16, main32, early, rim32, rim_pack, rims, edge_lo, edge_hi, west_hi, east_lo, depth_west, depth_east,
     wheres, fore, halo, cells, picks, picked, transform, result, back, out32, local_sem,
-    side_send, side_recv, where_send, where_recv, cell_send, cell_recv,
+    rim_send, rim_recv, side_send, side_recv, where_send, where_recv, cell_send, cell_recv,
     pick_send, pick_recv, back_send, back_recv,
 ):
     me = lax.axis_index("mem")
@@ -151,6 +151,12 @@
     for copy in local_copies:
         copy.start()
 
+    per = min(rows, 128 // EDGE)
+    at = iota((1, 2 * per * EDGE), 1)
+    inner = lax.rem(at, per * EDGE)
+    source = (inner // EDGE) * strip + lax.rem(inner, EDGE) + (at // (per * EDGE)) * (strip - EDGE)
+    choose = jnp.where(iota((per * strip, 2 * per * EDGE), 0) == source, 1.0, 0.0).astype(jnp.bfloat16)
+
     local_copies[0].wait()
     tall32[...] = x_ref[...].reshape(group * stack, strip).astype(jnp.float32)
     for c in range(3):
@@ -158,11 +164,6 @@
             row = tall32[pl.ds(c * rows + r, group, stride=stack), :]
             flat16[pl.ds(c * group, group), pl.ds(r * strip, strip)] = row.astype(jnp.bfloat16)
 
-    per = min(rows, 128 // EDGE)
-    at = iota((1, 2 * per * EDGE), 1)
-    inner = lax.rem(at, per * EDGE)
-    source = (inner // EDGE) * strip + lax.rem(inner, EDGE) + (at // (per * EDGE)) * (strip - EDGE)
-    choose = jnp.where(iota((per * strip, 2 * per * EDGE), 0) == source, 1.0, 0.0).astype(jnp.bfloat16)
     for t in range(rows // per):
         part = jnp.dot(
             flat16[:, pl.ds(t * per * strip, per * strip)], choose, preferred_element_type=jnp.float32
@@ -209,6 +210,16 @@
         for c, field in enumerate(forecast_rows(*state, depth)):
             for r in range(rows):
                 main32[c * rows + r, some, :] = field[r]
+                if c == 0:
+                    early[r // BAND, some, pl.ds((r % BAND) * strip, strip)] = field[r].astype(jnp.bfloat16)
+
+    def cell_copy(src, c, mask):
+        return to_mem(src, cells.at[c, me], cell_send.at[c, mask], cell_recv.at[c, mask], mask)
+
+    cell_copies = [[cell_copy(early.at[peers[mask]], 0, mask) for mask in masks]]
+    cell_copies += [[cell_copy(fore.at[peers[mask], c], c, mask) for mask in masks] for c in range(1, 3)]
+    for copy in cell_copies[0]:
+        copy.start()
 
     own_lo = pack_depth(depth_ref[...], 0, strip)
     own_hi = pack_depth(depth_ref[...], 1, strip)
@@ -235,6 +246,8 @@
             outer = jnp.where(place >= MARGIN_WIDTH, w_left[c], e_right[c])
             halo[pl.ds(pl.multiple_of(c * group + begin, CHUNK), CHUNK), :] = outer.astype(jnp.bfloat16)
             rim = jnp.where(place < MARGIN_WIDTH, w_right[c], e_left[c])
+            if c == 0:
+                rim32[some, :] = rim
             for t in range(rows // per):
                 tile = rim[:, t * per * EDGE : (t + 1) * per * EDGE]
                 turned = [tile] + [pltpu.roll(tile, (per - q) * EDGE, 1) for q in range(1, per)]
@@ -245,14 +258,22 @@
                     value = jnp.where(column >= strip - MARGIN_WIDTH, turned[(q + 1) % per], value)
                     fore[r // BAND, c, some, pl.ds((r % BAND) * strip, strip)] = value.astype(jnp.bfloat16)
 
-    cell_copies = [
-        [
-            to_mem(fore.at[peers[mask], c], cells.at[c, me], cell_send.at[c, mask], cell_recv.at[c, mask], mask)
-            for mask in masks
-        ]
-        for c in range(3)
+    segment = BAND * EDGE
+    tile = per * EDGE
+    at = iota((1, tile), 1)
+    for band in range(n):
+        total = jnp.zeros((CHUNK, tile), jnp.float32)
+        begin = band * segment
+        for q in range(group // CHUNK):
+            piece = rim32[q * CHUNK : (q + 1) * CHUNK, begin // tile * tile : (begin // tile + 1) * tile]
+            by = (q * segment - begin) % tile
+            piece = pltpu.roll(piece, by, 1) if by else piece
+            total = jnp.where(at // segment == q, piece, total)
+        rim_pack[band] = total.astype(jnp.bfloat16)
+    rim_copies = [
+        to_mem(rim_pack.at[peers[mask]], rims.at[me], rim_send.at[mask], rim_recv.at[mask], mask) for mask in masks
     ]
-    for copy in cell_copies[0]:
+    for copy in rim_copies:
         copy.start()
 
     for copy in where_copies:
@@ -301,6 +322,21 @@
     for c in range(3):
         cells[c, me] = fore[me, c]
 
+    column = iota((1, strip), 1)
+    for copy, rim_copy, mask in zip(cell_copies[0], rim_copies, masks):
+        copy.wait_recv()
+        rim_copy.wait_recv()
+        piece = rims[peers[mask]].astype(jnp.float32)
+        for q in range(group // CHUNK):
+            shifts = [(-(q * segment + b * EDGE)) % tile for b in range(BAND + 1)]
+            turned = [pltpu.roll(piece, by, 1) if by else piece for by in shifts]
+            for b in range(BAND):
+                some = (0, peers[mask], pl.ds(q * CHUNK, CHUNK), pl.ds(b * strip, strip))
+                value = cells[some].astype(jnp.float32)
+                value = jnp.where(column < MARGIN_WIDTH, turned[b], value)
+                value = jnp.where(column >= strip - MARGIN_WIDTH, turned[b + 1], value)
+                cells[some] = value.astype(jnp.bfloat16)
+
     for copy in local_copies[3:]:
         copy.wait()
     live = jnp.where(iota((1, slots), 1) < count_ref[...], 1.0, 0.0)
@@ -348,8 +384,9 @@
 
     back_copies = []
     for c in range(3):
-        for copy in cell_copies[c]:
-            copy.wait_recv()
+        if c > 0:
+            for copy in cell_copies[c]:
+                copy.wait_recv()
         all_cells = cells[c].reshape(members, cell)
         total = jnp.dot(transform[0], all_cells, preferred_element_type=jnp.float32)
         total += jnp.dot(transform[1], all_cells, preferred_element_type=jnp.float32)
@@ -375,7 +412,7 @@
             place_rows(c, peers[mask])
         out_ref[:, c, 0] = out32[c].reshape(group, rows, strip).astype(jnp.bfloat16)
 
-    for copy in side_copies + where_copies + pick_copies:
+    for copy in side_copies + where_copies + pick_copies + rim_copies:
         copy.wait_send()
     for c in range(3):
         for copy in cell_copies[c] + back_copies[c]:
@@ -408,6 +445,10 @@
         pltpu.VMEM((group * 3 * rows, strip), f32),
         pltpu.VMEM((3 * group, rows * strip), bf16),
         pltpu.VMEM((3 * rows, group, strip), f32),
+        pltpu.VMEM((n, group, cell), bf16),
+        pltpu.VMEM((group, lanes), f32),
+        pltpu.VMEM((n, CHUNK, min(lanes, 128)), bf16),
+        pltpu.VMEM((n, CHUNK, min(lanes, 128)), bf16),
     ]
     scratch += [pltpu.VMEM((3 * group, lanes), bf16)] * 4
     scratch += [pltpu.VMEM((rows, strip), f32)] * 2
@@ -424,7 +465,7 @@
         pltpu.VMEM((3, group * rows, strip), f32),
     ]
     scratch += [dma((7,))]
-    scratch += [dma((4,))] * 2 + [dma((n,))] * 2 + [dma((3, n))] * 2 + [dma((n,))] * 2 + [dma((3, n))] * 2
+    scratch += [dma((n,))] * 2 + [dma((4,))] * 2 + [dma((n,))] * 2 + [dma((3, n))] * 2 + [dma((n,))] * 2 + [dma((3, n))] * 2
     out = pl.pallas_call(
         functools.partial(kernel, n, lons),
         out_shape=pltpu.VMEM(sample_collection.shape, bf16),

time: 54.8 us -> 50.8 us (0.927)
  Pallas kernels: 54 us -> 50 us
    pallas_call x1, Pallas kernels: 53.1 us -> 49.1 us  [on_device(): pl.pallas_call(functools.partial(kernel, n, lons), out_shape=pltpu.VMEM(s...]
where the time goes in v2:
time: 50.8 us; the launch traced here: 50.6 us
  Pallas kernels  50 us (98%)
  between operations  0.66 us (1%)
    pallas_call x1, Pallas kernels, on_device(): pl.pallas_call(functools.partial(kernel, n, lons), out_shape=pltpu.VMEM(s...  49.1 us

profile of v2, /device:TPU:0, one launch (start us, length us, event | category | flops | bytes accessed | tf_op | source)
XLA Modules:
  0.0 50.6 jit_solution(15091669899677971462)
XLA Ops:
  0.7 49.1 %shard_map.73.in_ref = bf16[64,3,1,16,128]{4,3,2,1,0:T(8,128)(2,1)S(1)} custom-call(bf16[64,3,1,16,128]{4,3,2,1,0:T(8,128)(2,1)} %x_hbm.1, f32[16,128]{1,0:T(8,128)} %bitcast.5, s32[1,512]{1,0:T(1,128)} %bitcast.6, f32[1,512]{1,0:T(1,128)} %bitcast.7, f32[1,512]{1,0:T(1,128)} %bitcast.8, s32[1,512]{1,0:T(1,128)} %bitcast.9, s32[1,1]{1,0:T(1,128)S(6)} %copy.8.count_hbm), custom_call_target="tpu_custom_call" | custom-call | tf_op jit(solution)/shard_map/pallas_call | solution.py:469
  49.7 0.9 %shard_map.74 = bf16[64,3,1,16,128]{4,3,2,1,0:T(8,128)(2,1)} custom-call(bf16[64,3,1,16,128]{4,3,2,1,0:T(8,128)(2,1)S(1)} %shard_map.73.in_ref), custom_call_target="tpu_custom_call" | custom-call | tf_op jit(solution)/shard_map/pallas_call | solution.py:482

commit v3 on v2

--- a/solution.py
+++ b/solution.py
@@ -116,7 +116,7 @@
     x_hbm, depth_hbm, where_hbm, values_hbm, precision_hbm, loc_hbm, count_hbm, out_ref,
     x_ref, depth_ref, values_ref, precision_ref, loc_ref, count_ref, tall32, flat16, main32, early, rim32, rim_pack, rims, edge_lo, edge_hi, west_hi, east_lo, depth_west, depth_east,
     wheres, fore, halo, cells, picks, picked, transform, result, back, out32, local_sem,
-    rim_send, rim_recv, side_send, side_recv, where_send, where_recv, cell_send, cell_recv,
+    early_send, early_recv, rim_send, rim_recv, side_send, side_recv, where_send, where_recv, cell_send, cell_recv,
     pick_send, pick_recv, back_send, back_recv,
 ):
     me = lax.axis_index("mem")
@@ -132,7 +132,7 @@
     cell = BAND * strip
     lanes = rows * EDGE
     stack = 3 * rows
-    masks = list(range(n - 1, 0, -1))
+    masks = sorted(range(1, n), key=lambda mask: (mask.bit_count(), -mask))
     peers = {mask: xor(me, mask) for mask in masks}
     local_copies = [
         pltpu.make_async_copy(src, dst, local_sem.at[i])
@@ -198,6 +198,12 @@
         copy.start()
 
     local_copies[1].wait()
+
+    def early_copy(i, mask):
+        some = pl.ds(pl.multiple_of(i * CHUNK, CHUNK), CHUNK)
+        return to_mem(
+            early.at[peers[mask], some], cells.at[0, me, some], early_send.at[i, mask], early_recv.at[i, mask], mask
+        )
 
     @pl.loop(0, group // CHUNK)
     def _(i):
@@ -212,14 +218,8 @@
                 main32[c * rows + r, some, :] = field[r]
                 if c == 0:
                     early[r // BAND, some, pl.ds((r % BAND) * strip, strip)] = field[r].astype(jnp.bfloat16)
-
-    def cell_copy(src, c, mask):
-        return to_mem(src, cells.at[c, me], cell_send.at[c, mask], cell_recv.at[c, mask], mask)
-
-    cell_copies = [[cell_copy(early.at[peers[mask]], 0, mask) for mask in masks]]
-    cell_copies += [[cell_copy(fore.at[peers[mask], c], c, mask) for mask in masks] for c in range(1, 3)]
-    for copy in cell_copies[0]:
-        copy.start()
+        for mask in masks:
+            early_copy(i, mask).start()
 
     own_lo = pack_depth(depth_ref[...], 0, strip)
     own_hi = pack_depth(depth_ref[...], 1, strip)
@@ -258,6 +258,15 @@
                     value = jnp.where(column >= strip - MARGIN_WIDTH, turned[(q + 1) % per], value)
                     fore[r // BAND, c, some, pl.ds((r % BAND) * strip, strip)] = value.astype(jnp.bfloat16)
 
+    cell_copies = [
+        [
+            to_mem(fore.at[peers[mask], c], cells.at[c, me], cell_send.at[c, mask], cell_recv.at[c, mask], mask)
+            for mask in masks
+        ]
+        for c in range(1, 3)
+    ]
+    early_copies = {mask: [early_copy(i, mask) for i in range(group // CHUNK)] for mask in masks}
+
     segment = BAND * EDGE
     tile = per * EDGE
     at = iota((1, tile), 1)
@@ -276,6 +285,8 @@
     for copy in rim_copies:
         copy.start()
 
+    for copy in cell_copies[0][:1]:
+        copy.start()
     for copy in where_copies:
         copy.wait_recv()
     local_copies[2].wait()
@@ -316,15 +327,15 @@
         else:
             picked[me] = total.astype(jnp.bfloat16)
 
-    for c in range(1, 3):
-        for copy in cell_copies[c]:
-            copy.start()
+    for copy in cell_copies[0][1:] + cell_copies[1]:
+        copy.start()
     for c in range(3):
         cells[c, me] = fore[me, c]
 
     column = iota((1, strip), 1)
-    for copy, rim_copy, mask in zip(cell_copies[0], rim_copies, masks):
-        copy.wait_recv()
+    for rim_copy, mask in zip(rim_copies, masks):
+        for copy in early_copies[mask]:
+            copy.wait_recv()
         rim_copy.wait_recv()
         piece = rims[peers[mask]].astype(jnp.float32)
         for q in range(group // CHUNK):
@@ -385,7 +396,7 @@
     back_copies = []
     for c in range(3):
         if c > 0:
-            for copy in cell_copies[c]:
+            for copy in cell_copies[c - 1]:
                 copy.wait_recv()
         all_cells = cells[c].reshape(members, cell)
         total = jnp.dot(transform[0], all_cells, preferred_element_type=jnp.float32)
@@ -414,8 +425,8 @@
 
     for copy in side_copies + where_copies + pick_copies + rim_copies:
         copy.wait_send()
-    for c in range(3):
-        for copy in cell_copies[c] + back_copies[c]:
+    for row_copies in cell_copies + back_copies + list(early_copies.values()):
+        for copy in row_copies:
             copy.wait_send()
 
 
@@ -465,7 +476,7 @@
         pltpu.VMEM((3, group * rows, strip), f32),
     ]
     scratch += [dma((7,))]
-    scratch += [dma((n,))] * 2 + [dma((4,))] * 2 + [dma((n,))] * 2 + [dma((3, n))] * 2 + [dma((n,))] * 2 + [dma((3, n))] * 2
+    scratch += [dma((group // CHUNK, n))] * 2 + [dma((n,))] * 2 + [dma((4,))] * 2 + [dma((n,))] * 2 + [dma((3, n))] * 2 + [dma((n,))] * 2 + [dma((3, n))] * 2
     out = pl.pallas_call(
         functools.partial(kernel, n, lons),
         out_shape=pltpu.VMEM(sample_collection.shape, bf16),

time: 50.8 us -> 49.4 us (0.972)
  Pallas kernels: 50 us -> 48.6 us
    pallas_call x1, Pallas kernels: 49.1 us -> 47.7 us  [on_device(): pl.pallas_call(functools.partial(kernel, n, lons), out_shape=pltpu.VMEM(s...]
where the time goes in v3:
time: 49.4 us; the launch traced here: 49.2 us
  Pallas kernels  48.6 us (98%)
  between operations  0.66 us (1%)
    pallas_call x1, Pallas kernels, on_device(): pl.pallas_call(functools.partial(kernel, n, lons), out_shape=pltpu.VMEM(s...  47.7 us

profile of v3, /device:TPU:0, one launch (start us, length us, event | category | flops | bytes accessed | tf_op | source)
XLA Modules:
  0.0 49.2 jit_solution(4027294677927763302)
XLA Ops:
  0.7 47.7 %shard_map.73.in_ref = bf16[64,3,1,16,128]{4,3,2,1,0:T(8,128)(2,1)S(1)} custom-call(bf16[64,3,1,16,128]{4,3,2,1,0:T(8,128)(2,1)} %x_hbm.1, f32[16,128]{1,0:T(8,128)} %bitcast.5, s32[1,512]{1,0:T(1,128)} %bitcast.6, f32[1,512]{1,0:T(1,128)} %bitcast.7, f32[1,512]{1,0:T(1,128)} %bitcast.8, s32[1,512]{1,0:T(1,128)} %bitcast.9, s32[1,1]{1,0:T(1,128)S(6)} %copy.8.count_hbm), custom_call_target="tpu_custom_call" | custom-call | tf_op jit(solution)/shard_map/pallas_call | solution.py:480
  48.3 0.9 %shard_map.74 = bf16[64,3,1,16,128]{4,3,2,1,0:T(8,128)(2,1)} custom-call(bf16[64,3,1,16,128]{4,3,2,1,0:T(8,128)(2,1)S(1)} %shard_map.73.in_ref), custom_call_target="tpu_custom_call" | custom-call | tf_op jit(solution)/shard_map/pallas_call | solution.py:493
